TPU v7x, 32 devices: a whole 2x2x4 slice. The times are simulated.
32 devices in a mesh: dp: 8 (over z, x), fsdp: 4 (over y, core).
Axes of the slice: x: 2, y: 2, z: 4, core: 2. Of those that a mesh axis runs over, the one named last changes fastest.
Arguments:
- tokens: bfloat16 [32, 169, 1024], P(('dp', 'fsdp')), may hold values from -6 to 6
- out_grad: bfloat16 [32, 169, 1024], P(('dp', 'fsdp')), may hold values from -6 to 6
- text_len: int32 [32], P(('dp', 'fsdp')), may hold values from 12 to 120
- x_bucket: int32 [32, 169], P(('dp', 'fsdp')), may hold values from 0 to 127
- y_bucket: int32 [32, 169], P(('dp', 'fsdp')), may hold values from 0 to 127
- patch_mask: int32 [32, 49], P(('dp', 'fsdp')), may hold values 0 or 1
- qkv_weight: bfloat16 [1024, 3072], P(('dp', 'fsdp')), may hold values from -0.1875 to 0.1875
- qv_bias: bfloat16 [2048], P(('dp', 'fsdp')), may hold values from -3 to 3
- proj_weight: bfloat16 [1024, 1024], P(('dp', 'fsdp')), may hold values from -1 to 1
- proj_bias: bfloat16 [1024], P(('dp', 'fsdp')), may hold values from -2 to 2
- first_gain: bfloat16 [1024], P(('dp', 'fsdp')), may hold values from 0.5 to 1.5
- first_shift: bfloat16 [1024], P(('dp', 'fsdp')), may hold values from -2 to 2
- rel_tables: bfloat16 [6144], P(('dp', 'fsdp')), may hold values from -4 to 4
- up_weight: bfloat16 [1024, 4096], P(('dp', 'fsdp')), may hold values from -0.1875 to 0.1875
- up_bias: bfloat16 [4096], P(('dp', 'fsdp')), may hold values from -3 to 3
- down_weight: bfloat16 [1024, 4096], P(('dp', 'fsdp')), may hold values from -0.09375 to 0.09375
- down_bias: bfloat16 [1024], P(('dp', 'fsdp')), may hold values from -2 to 2
- second_gain: bfloat16 [1024], P(('dp', 'fsdp')), may hold values from 0.5 to 1.5
- second_shift: bfloat16 [1024], P(('dp', 'fsdp')), may hold values from -2 to 2
Outputs:
- encoded: bfloat16 [32, 169, 1024], P(('dp', 'fsdp'))
- grad_tokens: float32 [32, 169, 1024], P(('dp', 'fsdp'))
- grad_qkv: float32 [1024, 3072], P(('dp', 'fsdp'))
- grad_qvbias: float32 [2048], P(('dp', 'fsdp'))
- grad_proj: float32 [1024, 1024], P(('dp', 'fsdp'))
- grad_projbias: float32 [1024], P(('dp', 'fsdp'))
- grad_firstgain: float32 [1024], P(('dp', 'fsdp'))
- grad_firstshift: float32 [1024], P(('dp', 'fsdp'))
- grad_tables: float32 [6144], P(('dp', 'fsdp'))
- grad_up: float32 [1024, 4096], P(('dp', 'fsdp'))
- grad_upbias: float32 [4096], P(('dp', 'fsdp'))
- grad_down: float32 [1024, 4096], P(('dp', 'fsdp'))
- grad_downbias: float32 [1024], P(('dp', 'fsdp'))
- grad_secondgain: float32 [1024], P(('dp', 'fsdp'))
- grad_secondshift: float32 [1024], P(('dp', 'fsdp'))
All inputs are finite; a program needn't handle non-finite values. No bound on the sum of `patch_mask` on one device may be relied on, other than what follows from the above.
Results may differ from a plain program's by a relative error of at most 0.015.
Values may be sent and summed in bfloat16 or wider, within the bound.
No kernel may reach another device: no remote copies, remote signals or barrier semaphores. Data moves between devices by JAX's collectives and lax.ppermute only.
A program may use at most 256 MiB of HBM per device.

v0:
```python
from functools import partial
import jax
import jax.numpy as jnp
from jax import lax
from jax.sharding import PartitionSpec as P

D = 1024
H = 16
HD = 64
FF = 4096
NB = 128
TEXT = 120
SLOTS = 169
HIGHEST = lax.Precision.HIGHEST
NEGATIVE = -1e30
EPSILON = 1e-05


def layer_norm(values, norm_gain, norm_shift):
    average = jnp.mean(values, axis=-1, keepdims=True)
    centred = values - average
    spread = jnp.mean(centred * centred, axis=-1, keepdims=True)
    return centred * lax.rsqrt(spread + EPSILON) * norm_gain + norm_shift


def key_valid(text_len, patch_mask):
    places = jnp.arange(TEXT, dtype=jnp.int32)
    text_part = places[None, :] < text_len[:, None]
    return jnp.concatenate([text_part, patch_mask > 0], axis=1)


def relative_table(buckets):
    indices = jnp.arange(buckets, dtype=jnp.int32)
    offsets = (
        jnp.clip(indices[None, :] - indices[:, None], -(buckets // 2), buckets // 2 - 1)
        + buckets // 2
    )
    return offsets[:, :, None] == indices[None, None, :]


def right_product(left, right):
    return lax.dot_general(
        left, right, (((1,), (1,)), ((), ())), preferred_element_type=jnp.float32
    )


def rows_product(left, right):
    return lax.dot_general(
        left, right, (((0,), (0,)), ((), ())), preferred_element_type=jnp.float32
    )


def local(
    tokens,
    out_grad,
    text_len,
    x_bucket,
    y_bucket,
    patch_mask,
    qkv_weight,
    qv_bias,
    proj_weight,
    proj_bias,
    first_gain,
    first_shift,
    rel_tables,
    up_weight,
    up_bias,
    down_weight,
    down_bias,
    second_gain,
    second_shift,
):
    f32 = jnp.float32
    bf16 = jnp.bfloat16
    qkv_full, proj_full, qv_full, projb_full, gain_one, shift_one, tables_full = (
        lax.all_gather(qkv_weight, ("dp", "fsdp"), axis=0, tiled=True),
        lax.all_gather(proj_weight, ("dp", "fsdp"), axis=0, tiled=True),
        lax.all_gather(qv_bias, ("dp", "fsdp"), axis=0, tiled=True),
        lax.all_gather(proj_bias, ("dp", "fsdp"), axis=0, tiled=True),
        lax.all_gather(first_gain, ("dp", "fsdp"), axis=0, tiled=True),
        lax.all_gather(first_shift, ("dp", "fsdp"), axis=0, tiled=True),
        lax.all_gather(rel_tables, ("dp", "fsdp"), axis=0, tiled=True),
    )
    up_full, down_full, upb_full, downb_full, gain_two, shift_two = (
        lax.all_gather(up_weight, ("dp", "fsdp"), axis=0, tiled=True),
        lax.all_gather(down_weight, ("dp", "fsdp"), axis=0, tiled=True),
        lax.all_gather(up_bias, ("dp", "fsdp"), axis=0, tiled=True),
        lax.all_gather(down_bias, ("dp", "fsdp"), axis=0, tiled=True),
        lax.all_gather(second_gain, ("dp", "fsdp"), axis=0, tiled=True),
        lax.all_gather(second_shift, ("dp", "fsdp"), axis=0, tiled=True),
    )
    doc_count = tokens.shape[0]
    row_total = doc_count * SLOTS
    valid_keys = key_valid(text_len, patch_mask)
    row_keep = valid_keys.reshape(row_total, 1).astype(f32)
    key_mask = valid_keys[:, None, :]
    positions = jnp.arange(SLOTS, dtype=jnp.int32) * NB // SLOTS
    position_ids = positions[None, :]
    all_ids = jnp.stack([position_ids, x_bucket, y_bucket], axis=2)
    buckets = jnp.arange(NB, dtype=jnp.int32)
    one_hot = (all_ids[..., None] == buckets).astype(bf16)
    key_codes = one_hot.reshape(doc_count, SLOTS, 3 * NB)
    relation = relative_table(NB)
    table_grid = tables_full.reshape(3, H, NB)
    toeplitz = jnp.einsum(
        "khr,abr->khab", table_grid, relation.astype(bf16), preferred_element_type=f32
    ).astype(bf16)
    query_codes = (
        jnp.einsum("dika,khab->hdikb", one_hot, toeplitz, preferred_element_type=f32)
        .astype(bf16)
        .reshape(H, doc_count, SLOTS, 3 * NB)
    )
    rows_in = tokens.reshape(row_total, D)
    qkv_bias = jnp.concatenate(
        [qv_full[:D].astype(f32), jnp.zeros((D,), f32), qv_full[D:].astype(f32)]
    )
    qkv_rows = (jnp.dot(rows_in, qkv_full, preferred_element_type=f32) + qkv_bias).astype(bf16)
    head_major = qkv_rows.reshape(doc_count, SLOTS, 3, H, HD).transpose(2, 3, 0, 1, 4)
    queries = head_major[0]
    keys_all = head_major[1]
    values_all = head_major[2]

    def scores_for(query_h, key_h, code_h):
        content = jnp.einsum("die,dje->dij", query_h, key_h, preferred_element_type=f32) * 0.125
        spatial = jnp.einsum("dic,djc->dij", code_h, key_codes, preferred_element_type=f32)
        return jnp.where(key_mask, content + spatial, NEGATIVE)

    def attend(inputs):
        query_h, key_h, value_h, code_h = inputs
        scores = scores_for(query_h, key_h, code_h)
        row_peak = jnp.max(scores, axis=-1, keepdims=True)
        exponent = jnp.exp(scores - row_peak)
        row_sum = jnp.sum(exponent, axis=-1, keepdims=True)
        probs_low = (exponent / row_sum).astype(bf16)
        mixed_h = jnp.einsum("dij,dje->die", probs_low, value_h, preferred_element_type=f32).astype(
            bf16
        )
        return (mixed_h, (row_peak + jnp.log(row_sum))[..., 0])

    head_out, log_norm = lax.map(attend, (queries, keys_all, values_all, query_codes))
    attended = head_out.transpose(1, 2, 0, 3).reshape(row_total, D)
    branch = jnp.dot(attended, proj_full, preferred_element_type=f32) + projb_full.astype(f32)
    resid_one = rows_in.astype(f32) + branch
    gain_onef = gain_one.astype(f32)
    shift_onef = shift_one.astype(f32)
    normed_one = layer_norm(resid_one, gain_onef, shift_onef)
    normed_low = normed_one.astype(bf16)
    pre_act = jnp.dot(normed_low, up_full, preferred_element_type=f32) + upb_full.astype(f32)
    act_low = jax.nn.gelu(pre_act, approximate=False).astype(bf16)
    ffn_out = right_product(act_low, down_full) + downb_full.astype(f32)
    resid_two = normed_one + ffn_out
    gain_twof = gain_two.astype(f32)
    shift_twof = shift_two.astype(f32)
    final_rows = layer_norm(resid_two, gain_twof, shift_twof) * row_keep
    encoded = final_rows.astype(bf16).reshape(doc_count, SLOTS, D)
    qkv_back, proj_back = (
        lax.all_gather(qkv_weight, ("dp", "fsdp"), axis=0, tiled=True),
        lax.all_gather(proj_weight, ("dp", "fsdp"), axis=0, tiled=True),
    )
    up_back, down_back = (
        lax.all_gather(up_weight, ("dp", "fsdp"), axis=0, tiled=True),
        lax.all_gather(down_weight, ("dp", "fsdp"), axis=0, tiled=True),
    )
    grad_rows = out_grad.reshape(row_total, D).astype(f32) * row_keep
    unused, norm_two_back = jax.vjp(layer_norm, resid_two, gain_twof, shift_twof)
    d_resid_two, d_gain_two, d_shift_two = norm_two_back(grad_rows)
    d_ffn = d_resid_two.astype(bf16)
    d_down_bias = jnp.sum(d_ffn, axis=0, dtype=f32)
    d_act = jnp.dot(d_ffn, down_back, preferred_element_type=f32)
    unused, gelu_back = jax.vjp(partial(jax.nn.gelu, approximate=False), pre_act)
    d_pre = gelu_back(d_act)[0].astype(bf16)
    d_up_bias = jnp.sum(d_pre, axis=0, dtype=f32)
    d_normed = d_resid_two + right_product(d_pre, up_back)
    unused, norm_one_back = jax.vjp(layer_norm, resid_one, gain_onef, shift_onef)
    d_resid_one, d_gain_one, d_shift_one = norm_one_back(d_normed)
    d_branch = d_resid_one.astype(bf16)
    d_proj_bias = jnp.sum(d_branch, axis=0, dtype=f32)
    d_attended = right_product(d_branch, proj_back).astype(bf16)
    d_heads = d_attended.reshape(doc_count, SLOTS, H, HD).transpose(2, 0, 1, 3)
    hot_float = one_hot.astype(f32)

    def attend_back(inputs):
        query_h, key_h, value_h, code_h, d_out_h, log_h = inputs
        scores = scores_for(query_h, key_h, code_h)
        probability = jnp.exp(scores - log_h[..., None])
        d_probs = jnp.einsum("die,dje->dij", d_out_h, value_h, preferred_element_type=f32)
        d_scores = (
            probability * (d_probs - jnp.sum(probability * d_probs, axis=-1, keepdims=True))
        ).astype(bf16)
        probs_low = probability.astype(bf16)
        d_value = jnp.einsum("dij,die->dje", probs_low, d_out_h, preferred_element_type=f32)
        d_query = jnp.einsum("dij,dje->die", d_scores, key_h, preferred_element_type=f32) * 0.125
        d_key = jnp.einsum("dij,die->dje", d_scores, query_h, preferred_element_type=f32) * 0.125
        d_codes = jnp.einsum(
            "dij,djc->dic", d_scores, key_codes, preferred_element_type=f32
        ).reshape(doc_count, SLOTS, 3, NB)
        d_grid = jnp.einsum("dika,dikb->kab", hot_float, d_codes, precision=HIGHEST)
        return ((d_query.astype(bf16), d_key.astype(bf16), d_value.astype(bf16)), d_grid)

    (d_query_all, d_key_all, d_value_all), d_grids = lax.map(
        attend_back, (queries, keys_all, values_all, query_codes, d_heads, log_norm)
    )
    d_qkv = (
        jnp.stack([d_query_all, d_key_all, d_value_all])
        .transpose(2, 3, 0, 1, 4)
        .reshape(row_total, 3 * D)
    )
    d_qv_bias = jnp.concatenate(
        [jnp.sum(d_qkv[:, :D], axis=0, dtype=f32), jnp.sum(d_qkv[:, 2 * D :], axis=0, dtype=f32)]
    )
    grad_tokens = d_resid_one + right_product(d_qkv, qkv_back)
    d_tables = jnp.einsum(
        "hkab,abr->khr", d_grids, relation.astype(f32), precision=HIGHEST
    ).reshape(3 * H * NB)
    outer_count = lax.axis_size("dp")
    inner_count = lax.axis_size("fsdp")
    block_rows = D // (outer_count * inner_count)
    columns = 4 * D + 2 * FF
    term = jnp.concatenate(
        [
            rows_product(rows_in, d_qkv),
            rows_product(attended, d_branch),
            rows_product(normed_low, d_pre),
            rows_product(d_ffn, act_low),
        ],
        axis=1,
    )
    arrived = lax.all_to_all(
        term.reshape(outer_count, D // outer_count, columns).astype(jnp.bfloat16),
        "dp",
        split_axis=0,
        concat_axis=0,
        tiled=True,
    ).astype(jnp.float32)
    outer_rows = jnp.sum(arrived, axis=0)
    arrived_inner = lax.all_to_all(
        outer_rows.reshape(inner_count, block_rows, columns).astype(jnp.bfloat16),
        "fsdp",
        split_axis=0,
        concat_axis=0,
        tiled=True,
    ).astype(jnp.float32)
    weight_rows = jnp.sum(arrived_inner, axis=0)
    grad_qkv = weight_rows[:, : 3 * D]
    grad_proj = weight_rows[:, 3 * D : 4 * D]
    grad_up = weight_rows[:, 4 * D : 4 * D + FF]
    grad_down = weight_rows[:, 4 * D + FF :]
    (
        grad_qvbias,
        grad_projbias,
        grad_firstgain,
        grad_firstshift,
        grad_tables,
        grad_upbias,
        grad_downbias,
        grad_secondgain,
        grad_secondshift,
    ) = (
        lax.psum_scatter(d_qv_bias, ("dp", "fsdp"), scatter_dimension=0, tiled=True),
        lax.psum_scatter(d_proj_bias, ("dp", "fsdp"), scatter_dimension=0, tiled=True),
        lax.psum_scatter(d_gain_one, ("dp", "fsdp"), scatter_dimension=0, tiled=True),
        lax.psum_scatter(d_shift_one, ("dp", "fsdp"), scatter_dimension=0, tiled=True),
        lax.psum_scatter(d_tables, ("dp", "fsdp"), scatter_dimension=0, tiled=True),
        lax.psum_scatter(d_up_bias, ("dp", "fsdp"), scatter_dimension=0, tiled=True),
        lax.psum_scatter(d_down_bias, ("dp", "fsdp"), scatter_dimension=0, tiled=True),
        lax.psum_scatter(d_gain_two, ("dp", "fsdp"), scatter_dimension=0, tiled=True),
        lax.psum_scatter(d_shift_two, ("dp", "fsdp"), scatter_dimension=0, tiled=True),
    )
    return (
        encoded,
        grad_tokens.reshape(doc_count, SLOTS, D),
        grad_qkv,
        grad_qvbias,
        grad_proj,
        grad_projbias,
        grad_firstgain,
        grad_firstshift,
        grad_tables,
        grad_up,
        grad_upbias,
        grad_down,
        grad_downbias,
        grad_secondgain,
        grad_secondshift,
    )


def solution(mesh):
    return jax.shard_map(
        local,
        mesh=mesh,
        in_specs=(
            P(("dp", "fsdp"), None, None),
            P(("dp", "fsdp"), None, None),
            P(("dp", "fsdp")),
            P(("dp", "fsdp"), None),
            P(("dp", "fsdp"), None),
            P(("dp", "fsdp"), None),
            P(("dp", "fsdp"), None),
            P(("dp", "fsdp")),
            P(("dp", "fsdp"), None),
            P(("dp", "fsdp")),
            P(("dp", "fsdp")),
            P(("dp", "fsdp")),
            P(("dp", "fsdp")),
            P(("dp", "fsdp"), None),
            P(("dp", "fsdp")),
            P(("dp", "fsdp"), None),
            P(("dp", "fsdp")),
            P(("dp", "fsdp")),
            P(("dp", "fsdp")),
        ),
        out_specs=(
            P(("dp", "fsdp"), None, None),
            P(("dp", "fsdp"), None, None),
            P(("dp", "fsdp"), None),
            P(("dp", "fsdp")),
            P(("dp", "fsdp"), None),
            P(("dp", "fsdp")),
            P(("dp", "fsdp")),
            P(("dp", "fsdp")),
            P(("dp", "fsdp")),
            P(("dp", "fsdp"), None),
            P(("dp", "fsdp")),
            P(("dp", "fsdp"), None),
            P(("dp", "fsdp")),
            P(("dp", "fsdp")),
            P(("dp", "fsdp")),
        ),
        check_vma=False,
    )
```

profile of v0, /device:TPU:8, one launch (start us, length us, event | category | flops | bytes accessed | tf_op | source)
XLA Modules:
  0.0 1361.8 jit_solution(18023036616747059392)
XLA Ops:
  18.1 41.5 %all-reduce.18 = (bf16[2048]{0:T(1024)(128)(2,1)S(1)}, bf16[6144]{0:T(1024)(128)(2,1)S(1)}, bf16[1024]{0:T(1024)(128)(2,1)S(1)}, bf16[1024]{0:T(1024)(128)(2,1)S...) all-reduce(bf16[2048]{0:T(1024)(128)(2,1)S(1)} %dynamic-update-slic, ...), channel_id=1, replica_groups=mesh['dp'=8,'fsdp'=4] {'dp','fsdp'}, use_global_device_ids=true, to_apply=%add | all-reduce | flops 14336 | bytes 57344
  59.7 34.3 %all-gather = bf16[32,1,128]{2,1,0:T(2,128)(2,1)S(1)} all-gather(bf16[1,1,128]{2,1,0:T(2,128)(2,1)} %bitcast.272), channel_id=1, replica_groups=mesh['dp'=8,'fsdp'=4] {'dp','fsdp'}, dimensions={0}, use_global_device_ids=true | all-gather | bytes 8448 | tf_op jit(solution)/shard_map/all_gather | solution.py:88
  120.6 45.8 %while.31 = (s32[]{:T(128)}, bf16[16,1,169,64]{2,3,1,0:T(8,128)(2,1)S(1)}, f32[16,1,169]{2,1,0:T(1,128)S(1)}, pred[1,1,169]{2,1,0:T(4,128)(4,1)S(1)}, bf16[16,1,...) while((s32[]{:T(128)}, ...), condition=%wide.region_3.4_spmd.clone, body=%wide.region_0.3_spmd.clone.sunk | while | flops 29643952 | bytes 1993045 | solution.py:141
  169.8 49.5 %all-gather.10.cloned.1.call-done = bf16[1024,4096]{1,0:T(8,128)(2,1)} async-done(((bf16[32,4096]{1,0:T(8,128)(2,1)}), bf16[1024,4096]{1,0:T(8,128)(2,1)}) %all-gather.10.cloned.1.call-update) | async-done | bytes 8388624 | tf_op jit(solution)/shard_map/all_gather | solution.py:86
  219.3 12.2 multiply_convert_fusion.1
  231.6 66.6 %all-gather.12.cloned.1.call-done = bf16[1024,4096]{1,0:T(8,128)(2,1)} async-done(((bf16[32,4096]{1,0:T(8,128)(2,1)}), bf16[1024,4096]{1,0:T(8,128)(2,1)}) %all-gather.12.cloned.1.call-update) | async-done | bytes 8388624 | tf_op jit(solution)/shard_map/all_gather | solution.py:87
  298.2 7.0 fusion.122
  335.2 262.0 %while.32 = (s32[]{:T(128)}, bf16[16,1,169,64]{2,3,1,0:T(8,128)(2,1)}, bf16[16,1,169,64]{2,3,1,0:T(8,128)(2,1)}, bf16[16,1,169,64]{2,3,1,0:T(8,128)(2,1)}, f32[1...) while((s32[]{:T(128)}, ...), condition=%wide.region_14.15_spmd.clone.clone, body=%wide.region_12.14_spmd.clone.clone.sunk | while | flops 162622784 | bytes 5006393 | solution.py:201
  345.1 6.5 dynamic_update_slice.47
  361.4 6.5 dynamic_update_slice.47
  426.9 6.5 dynamic_update_slice.47
  475.9 6.5 dynamic_update_slice.47
  492.3 6.5 dynamic_update_slice.47
  508.7 6.5 dynamic_update_slice.47
  525.1 6.5 dynamic_update_slice.47
  541.5 6.5 dynamic_update_slice.47
  557.9 6.5 dynamic_update_slice.47
  574.3 6.5 dynamic_update_slice.47
  590.7 6.5 dynamic_update_slice.47
  606.0 8.7 copy.122
  614.7 17.5 %pad_maximum_fusion = bf16[1024,12288]{1,0:T(8,128)(2,1)} fusion(bf16[1024,4096]{1,0:T(8,128)(2,1)} %convolution_convert_fusion.2, bf16[1024,4096]{1,0:T(8,128)(2,1)} %convolution_convert_fusion.3, bf16[1024,1024]{1,0:T(8,128)(2,1)} %copy.123, bf16[1024,3072]{1,0:T(8,128)(2,1)} %copy.122), kind=kLoop, calls=%fused_computation.85 | loop fusion | flops 100663296 | bytes 50331648 | tf_op jit(solution)/shard_map/concatenate | solution.py:220
  632.2 552.2 %all_to_all.10 = bf16[8,128,12288]{2,1,0:T(8,128)(2,1)} all-to-all(bf16[8,128,12288]{2,1,0:T(8,128)(2,1)} %bitcast.252), channel_id=1, replica_groups=mesh['dp'=8,'fsdp'=4] {'dp'}, dimensions={0} | all-to-all | bytes 50331648 | tf_op jit(solution)/shard_map/all_to_all | solution.py:229
  1184.5 15.2 %reduce_sum.205 = bf16[128,12288]{1,0:T(8,128)(2,1)} reduce(bf16[8,128,12288]{2,1,0:T(8,128)(2,1)} %all_to_all.10, bf16[]{:T(256)} %constant.70.clone.1), dimensions={0}, to_apply=%region_15.16 | reduce | flops 11010048 | bytes 28311554 | tf_op jit(solution)/shard_map/reduce_sum | solution.py:236
  1218.3 120.3 %all-reduce.21.cloned.1.call-done = (f32[2048]{0:T(1024)}, f32[1024]{0:T(1024)}, f32[1024]{0:T(1024)}, f32[1024]{0:T(1024)}, f32[6144]{0:T(1024)}, /*index=5*/f3...) async-done(((f32[2048]{0:T(1024)}, f32[1024]{0:T(1024)}, f32[1024]{0:T(1024)}, f32[1024]{0:T(1024)}, f32[6144]{0:T(1024)}, /*index=5*/f32[4096]{0:T(1024)}, ...) | async-done | bytes 73744
  (563 shorter events, 348.1 us)
Async XLA Ops:
  7.2 101.6 %all-gather.6.cloned.1.call-start = ((), (), s32[]{:S(2)}) async-start(), calls=%async_computation.2 | async-start | bytes 6488064 | tf_op jit(solution)/shard_map/all_gather | solution.py:77
  7.9 158.6 %all-gather.8.cloned.1.call-start = ((), (), s32[]{:S(2)}) async-start(), calls=%async_computation.3 | async-start | bytes 2162688 | tf_op jit(solution)/shard_map/all_gather | solution.py:78
  8.7 210.6 %all-gather.10.cloned.1.call-start = ((), (), s32[]{:S(2)}) async-start(), calls=%async_computation.4 | async-start | bytes 8650752 | tf_op jit(solution)/shard_map/all_gather | solution.py:86
  9.4 288.8 %all-gather.12.cloned.1.call-start = ((), (), s32[]{:S(2)}) async-start(), calls=%async_computation.5 | async-start | bytes 8650752 | tf_op jit(solution)/shard_map/all_gather | solution.py:87
  103.1 5.7 copy-start.7
  166.5 65.1 %copy-start.3 = (bf16[16,1,169,64]{2,3,1,0:T(8,128)(2,1)}, bf16[16,1,169,64]{2,3,1,0:T(8,128)(2,1)S(1)}, u32[]{:S(2)}) copy-start(bf16[16,1,169,64]{2,3,1,0:T(8,128)(2,1)S(1)} %get-tuple-element.138) | copy-start | bytes 1038340
  166.5 65.1 %copy-start.5 = (bf16[16,1,169,64]{3,2,1,0:T(8,128)(2,1)}, bf16[16,1,169,64]{3,2,1,0:T(8,128)(2,1)S(1)}, u32[]{:S(2)}) copy-start(bf16[16,1,169,64]{3,2,1,0:T(8,128)(2,1)S(1)} %get-tuple-element.782) | copy-start | bytes 1038340
  166.5 65.1 %copy-start.6 = (bf16[16,1,169,64]{3,2,1,0:T(8,128)(2,1)}, bf16[16,1,169,64]{3,2,1,0:T(8,128)(2,1)S(1)}, u32[]{:S(2)}) copy-start(bf16[16,1,169,64]{3,2,1,0:T(8,128)(2,1)S(1)} %get-tuple-element.783) | copy-start | bytes 1038340
  298.2 7.3 copy-start.9
  298.2 15.8 %slice-start.2 = ((s8[8388608]{0:T(1024)(128)(4,1)}), s8[4194304]{0:T(1024)(128)(4,1)S(1)}, s32[]{:S(2)}) async-start(s8[8388608]{0:T(1024)(128)(4,1)} %bitcast.275), calls=%async_computation.9 | async-start | bytes 8388608
  305.3 3.1 copy-start.10
  306.5 7.5 slice-start.3
  308.4 5.6 copy-start.11
  308.4 16.6 %slice-start = ((s8[8388608]{0:T(1024)(128)(4,1)}), s8[4194304]{0:T(1024)(128)(4,1)S(1)}, s32[]{:S(2)}) async-start(s8[8388608]{0:T(1024)(128)(4,1)} %bitcast.273), calls=%async_computation.7 | async-start | bytes 8388608
  314.0 11.0 slice-start.1
  328.8 1.2 copy-start.4
  328.8 2.0 copy-start
  329.1 0.9 copy-start.1
  599.8 1.8 copy-start.8
  1199.7 150.3 %all-to-all-start.1 = ((bf16[4,32,12288]{2,1,0:T(8,128)(2,1)}), bf16[4,32,12288]{2,1,0:T(8,128)(2,1)}, u32[]{:S(2)}, u32[]{:S(2)}) async-start(bf16[4,32,12288]{2,1,0:T(8,128)(2,1)} %bitcast.256), calls=%async_computation.1 | async-start | bytes 6291456 | tf_op jit(solution)/shard_map/all_to_all | solution.py:237
  1204.3 134.2 %all-reduce.21.cloned.1.call-start = ((), (), s32[]{:S(2)}) async-start(), calls=%async_computation.6 | async-start | bytes 147456
  1205.6 6.1 copy-start.2
Sparse Core Ops, SparseCore 0:
  10.9 70.7 all-gather.5
  84.6 54.3 all-gather.7
  141.9 77.3 all-gather.9
  222.0 76.1 all-gather.11
  1212.4 126.0 all-reduce.20
where the time goes:
time: 1370 us; the launch traced here: 1360 us
  blocking collectives  628 us (46%)
  matrix products  252 us (18%)
  waiting for transfers between devices  239 us (17%)
  local copies, waits for them, and re-layouts  175 us (13%)
  other arithmetic  46.6 us (3%)
  between operations  15.1 us (1%)
    all_to_all x1, blocking collectives, local(): lax.all_to_all(term.reshape(outer_count, D // outer_count, columns).astyp...  552 us
    unnamed x6, waiting for transfers between devices  123 us
    dynamic_update_slice x32, local copies, waits for them, and re-layouts, local(): lax.map(attend_back, (queries, keys_all, values_all, query_codes, d_heads...  106 us
    all_gather x1, waiting for transfers between devices, local(): lax.all_gather(down_weight, ('dp', 'fsdp'), axis=0, tiled=True)  66.6 us
    all_gather x1, waiting for transfers between devices, local(): lax.all_gather(up_weight, ('dp', 'fsdp'), axis=0, tiled=True)  49.5 us
    unnamed x1, blocking collectives  41.5 us
    dot_general x32, matrix products, scores_for(): jnp.einsum('dic,djc->dij', code_h, key_codes, preferred_element_type=f32)  37 us
    all_gather x1, blocking collectives, local(): lax.all_gather(up_bias, ('dp', 'fsdp'), axis=0, tiled=True)  34.3 us
  transfers between devices with their start and end apart: 6, of which 3 were waited for; matrix products, arithmetic and copies ran while one was open for 9% of the time, Pallas kernels for 0%

commit v1 on v0

--- a/solution.py
+++ b/solution.py
@@ -14,6 +14,18 @@
 HIGHEST = lax.Precision.HIGHEST
 NEGATIVE = -1e30
 EPSILON = 1e-05
+
+
+def gather_by_bits(shard, axis, dim):
+    ways, here = (lax.axis_size(axis), lax.axis_index(axis))
+    grown, reach = (shard, 1)
+    while reach < ways:
+        theirs = lax.ppermute(grown, axis, [(d, d ^ reach) for d in range(ways)])
+        mine_first = jnp.concatenate([grown, theirs], axis=dim)
+        theirs_first = jnp.concatenate([theirs, grown], axis=dim)
+        grown = jnp.where(here & reach == 0, mine_first, theirs_first)
+        reach = 2 * reach
+    return grown
 
 
 def layer_norm(values, norm_gain, norm_shift):
@@ -83,7 +95,7 @@
         lax.all_gather(rel_tables, ("dp", "fsdp"), axis=0, tiled=True),
     )
     up_full, down_full, upb_full, downb_full, gain_two, shift_two = (
-        lax.all_gather(up_weight, ("dp", "fsdp"), axis=0, tiled=True),
+        gather_by_bits(up_weight, ("dp", "fsdp"), 0),
         lax.all_gather(down_weight, ("dp", "fsdp"), axis=0, tiled=True),
         lax.all_gather(up_bias, ("dp", "fsdp"), axis=0, tiled=True),
         lax.all_gather(down_bias, ("dp", "fsdp"), axis=0, tiled=True),

time: 1370 us -> 1530 us (1.12)
  waiting for transfers between devices: 239 us -> 322 us
  blocking collectives: 628 us -> 669 us
    ppermute x0 -> x5, waiting for transfers between devices: none -> 184 us  [gather_by_bits(): theirs = lax.ppermute(grown, axis, [(d, d ^ reach) for d in range(ways)])]
    all_gather x1, waiting for transfers between devices: 66.6 us -> 0.02 us  [local(): lax.all_gather(down_weight, ('dp', 'fsdp'), axis=0, tiled=True)]
    unnamed x1, blocking collectives: 41.5 us -> 82.5 us
    all_gather x1, waiting for transfers between devices: 49.5 us -> 16 us  [local(): lax.all_gather(up_weight, ('dp', 'fsdp'), axis=0, tiled=True)]
    unnamed x64 -> x96, local copies, waits for them, and re-layouts: 32.9 us -> 28.1 us
  transfers between devices with their start and end apart: 6 -> 11, of which waited for: 3 -> 6; matrix products, arithmetic and copies ran while one was open for 9% -> 11% of each run, Pallas kernels for 0% -> 0%
where the time goes in v1:
time: 1530 us; the launch traced here: 1520 us
  blocking collectives  669 us (44%)
  waiting for transfers between devices  322 us (21%)
  matrix products  255 us (17%)
  local copies, waits for them, and re-layouts  190 us (12%)
  other arithmetic  57.4 us (4%)
  between operations  15.3 us (1%)
    all_to_all x1, blocking collectives, local(): lax.all_to_all(term.reshape(outer_count, D // outer_count, columns).astyp...  552 us
    ppermute x5, waiting for transfers between devices, gather_by_bits(): theirs = lax.ppermute(grown, axis, [(d, d ^ reach) for d in range(ways)])  184 us
    unnamed x6, waiting for transfers between devices  122 us
    dynamic_update_slice x32, local copies, waits for them, and re-layouts, local(): lax.map(attend_back, (queries, keys_all, values_all, query_codes, d_heads...  106 us
    unnamed x1, blocking collectives  82.5 us
    dot_general x32, matrix products, scores_for(): jnp.einsum('dic,djc->dij', code_h, key_codes, preferred_element_type=f32)  37.1 us
    all_gather x1, blocking collectives, local(): lax.all_gather(up_bias, ('dp', 'fsdp'), axis=0, tiled=True)  34.1 us
  transfers between devices with their start and end apart: 11, of which 6 were waited for; matrix products, arithmetic and copies ran while one was open for 11% of the time, Pallas kernels for 0%

profile of v1, /device:TPU:8, one launch (start us, length us, event | category | flops | bytes accessed | tf_op | source)
XLA Modules:
  0.0 1519.0 jit_solution(12575823538123700840)
XLA Ops:
  14.1 13.8 collective-permute-done.1
  29.6 28.6 %collective-permute-done.2 = bf16[128,4096]{1,0:T(8,128)(2,1)} collective-permute-done((bf16[128,4096]{1,0:T(8,128)(2,1)S(1)}, bf16[128,4096]{1,0:T(8,128)(2,1)}, u32[]{:S(2)}, u32[]{:S(2)}) %collective-permute-start.2) | collective-permute-done | bytes 1048608 | tf_op jit(solution)/shard_map/ppermute | solution.py:23
  63.8 82.5 %all-reduce.18 = (bf16[2048]{0:T(1024)(128)(2,1)S(1)}, bf16[6144]{0:T(1024)(128)(2,1)S(1)}, bf16[1024]{0:T(1024)(128)(2,1)S(1)}, bf16[1024]{0:T(1024)(128)(2,1)S...) all-reduce(bf16[2048]{0:T(1024)(128)(2,1)S(1)} %dynamic-update-slic, ...), channel_id=1, replica_groups=mesh['dp'=8,'fsdp'=4] {'dp','fsdp'}, use_global_device_ids=true, to_apply=%add | all-reduce | flops 14336 | bytes 57344
  146.9 34.1 %all-gather = bf16[32,1,128]{2,1,0:T(2,128)(2,1)S(1)} all-gather(bf16[1,1,128]{2,1,0:T(2,128)(2,1)S(1)} %bitcast.273), channel_id=1, replica_groups=mesh['dp'=8,'fsdp'=4] {'dp','fsdp'}, dimensions={0}, use_global_device_ids=true | all-gather | bytes 8448 | tf_op jit(solution)/shard_map/all_gather | solution.py:100
  213.0 54.8 %while.31 = (s32[]{:T(128)}, bf16[16,1,169,64]{2,3,1,0:T(8,128)(2,1)S(1)}, f32[16,1,169]{2,1,0:T(1,128)}, pred[1,1,169]{2,1,0:T(4,128)(4,1)S(1)}, bf16[16,1,169,...) while((s32[]{:T(128)}, ...), condition=%wide.region_3.4_spmd.clone, body=%wide.region_0.3_spmd.clone.sunk | while | flops 29643952 | bytes 1992697 | solution.py:153
  271.0 140.2 %collective-permute-done.4 = bf16[512,4096]{1,0:T(8,128)(2,1)} collective-permute-done((bf16[512,4096]{1,0:T(8,128)(2,1)}, bf16[512,4096]{1,0:T(8,128)(2,1)}, u32[]{:S(2)}, u32[]{:S(2)}) %collective-permute-start.4) | collective-permute-done | bytes 4194336 | tf_op jit(solution)/shard_map/ppermute | solution.py:23
  411.3 14.7 multiply_convert_fusion.1
  426.1 7.0 fusion.131
  452.4 16.0 %all-gather.12.cloned.1.call-done = bf16[1024,4096]{1,0:T(8,128)(2,1)} async-done(((bf16[32,4096]{1,0:T(8,128)(2,1)}), bf16[1024,4096]{1,0:T(8,128)(2,1)}) %all-gather.12.cloned.1.call-update) | async-done | bytes 8388624 | tf_op jit(solution)/shard_map/all_gather | solution.py:174
  468.5 7.4 multiply_reduce_fusion.1
  482.3 272.6 %while.32 = (s32[]{:T(128)}, bf16[16,1,169,64]{2,3,1,0:T(8,128)(2,1)}, bf16[16,1,169,64]{2,3,1,0:T(8,128)(2,1)}, bf16[16,1,169,64]{2,3,1,0:T(8,128)(2,1)}, f32[1...) while((s32[]{:T(128)}, ...), condition=%wide.region_14.15_spmd.clone.clone, body=%wide.region_12.14_spmd.clone.clone.sunk | while | flops 162622784 | bytes 5006393 | solution.py:213
  628.9 6.5 dynamic_update_slice.47
  646.0 6.5 dynamic_update_slice.47
  663.0 6.5 dynamic_update_slice.47
  680.1 6.5 dynamic_update_slice.47
  697.2 6.5 dynamic_update_slice.47
  714.2 6.5 dynamic_update_slice.47
  731.3 6.5 dynamic_update_slice.47
  748.3 6.5 dynamic_update_slice.47
  763.7 8.7 copy.122
  772.3 17.5 %pad_maximum_fusion = bf16[1024,12288]{1,0:T(8,128)(2,1)} fusion(bf16[1024,4096]{1,0:T(8,128)(2,1)} %convolution_convert_fusion.2, bf16[1024,4096]{1,0:T(8,128)(2,1)} %convolution_convert_fusion.3, bf16[1024,1024]{1,0:T(8,128)(2,1)} %copy.123, bf16[1024,3072]{1,0:T(8,128)(2,1)} %copy.122), kind=kLoop, calls=%fused_computation.85 | loop fusion | flops 100663296 | bytes 50331648 | tf_op jit(solution)/shard_map/concatenate | solution.py:232
  789.9 552.2 %all_to_all.10 = bf16[8,128,12288]{2,1,0:T(8,128)(2,1)} all-to-all(bf16[8,128,12288]{2,1,0:T(8,128)(2,1)} %bitcast.251), channel_id=1, replica_groups=mesh['dp'=8,'fsdp'=4] {'dp'}, dimensions={0} | all-to-all | bytes 50331648 | tf_op jit(solution)/shard_map/all_to_all | solution.py:241
  1342.1 15.2 %reduce_sum.205 = bf16[128,12288]{1,0:T(8,128)(2,1)} reduce(bf16[8,128,12288]{2,1,0:T(8,128)(2,1)} %all_to_all.10, bf16[]{:T(256)} %constant.44.clone.1), dimensions={0}, to_apply=%region_15.16 | reduce | flops 11010048 | bytes 28311554 | tf_op jit(solution)/shard_map/reduce_sum | solution.py:248
  1376.1 119.7 %all-reduce.21.cloned.1.call-done = (f32[2048]{0:T(1024)}, f32[1024]{0:T(1024)}, f32[1024]{0:T(1024)}, f32[1024]{0:T(1024)}, f32[6144]{0:T(1024)}, /*index=5*/f3...) async-done(((f32[2048]{0:T(1024)}, f32[1024]{0:T(1024)}, f32[1024]{0:T(1024)}, f32[1024]{0:T(1024)}, f32[6144]{0:T(1024)}, /*index=5*/f32[4096]{0:T(1024)}, ...) | async-done | bytes 73744
  (609 shorter events, 392.5 us)
Async XLA Ops:
  7.2 195.2 %all-gather.6.cloned.1.call-start = ((), (), s32[]{:S(2)}) async-start(), calls=%async_computation.2 | async-start | bytes 6488064 | tf_op jit(solution)/shard_map/all_gather | solution.py:89
  7.9 259.9 %all-gather.8.cloned.1.call-start = ((), (), s32[]{:S(2)}) async-start(), calls=%async_computation.3 | async-start | bytes 2162688 | tf_op jit(solution)/shard_map/all_gather | solution.py:90
  8.7 417.4 %all-gather.10.cloned.1.call-start = ((), (), s32[]{:S(2)}) async-start(), calls=%async_computation.4 | async-start | bytes 8650752 | tf_op jit(solution)/shard_map/all_gather | solution.py:99
  9.4 459.1 %all-gather.12.cloned.1.call-start = ((), (), s32[]{:S(2)}) async-start(), calls=%async_computation.5 | async-start | bytes 8650752 | tf_op jit(solution)/shard_map/all_gather | solution.py:174
  9.4 1.8 collective-permute-start
  12.4 15.4 %collective-permute-start.1 = (bf16[64,4096]{1,0:T(8,128)(2,1)S(1)}, bf16[64,4096]{1,0:T(8,128)(2,1)S(1)}, u32[]{:S(2)}, u32[]{:S(2)}) collective-permute-start(bf16[64,4096]{1,0:T(8,128)(2,1)S(1)} %maximum_select_fusion.7), channel_id=1, source_target_pairs={{0,2},{1,3},{2,0},{3,1},{4,6},{5,7},{6,4},{7,5},{8,10},{9,11},{10,... | collective-permute-start | bytes 1572872 | tf_op jit(solution)/shard_map/ppermute | solution.py:23
  14.0 48.4 %copy-start.23 = (bf16[32]{0:T(256)(128)(2,1)S(1)}, bf16[32]{0:T(256)(128)(2,1)}, u32[]{:S(2)}) copy-start(bf16[32]{0:T(256)(128)(2,1)} %param.33) | copy-start | bytes 196
  14.0 48.6 %copy-start.24 = (bf16[32]{0:T(256)(128)(2,1)S(1)}, bf16[32]{0:T(256)(128)(2,1)}, u32[]{:S(2)}) copy-start(bf16[32]{0:T(256)(128)(2,1)} %param.34) | copy-start | bytes 196
  14.0 48.8 %copy-start.25 = (bf16[32]{0:T(256)(128)(2,1)S(1)}, bf16[32]{0:T(256)(128)(2,1)}, u32[]{:S(2)}) copy-start(bf16[32]{0:T(256)(128)(2,1)} %param.32) | copy-start | bytes 196
  14.0 49.0 %copy-start.26 = (bf16[32]{0:T(256)(128)(2,1)S(1)}, bf16[32]{0:T(256)(128)(2,1)}, u32[]{:S(2)}) copy-start(bf16[32]{0:T(256)(128)(2,1)} %param.40) | copy-start | bytes 196
  14.0 49.3 %copy-start.27 = (bf16[64]{0:T(256)(128)(2,1)S(1)}, bf16[64]{0:T(256)(128)(2,1)}, u32[]{:S(2)}) copy-start(bf16[64]{0:T(256)(128)(2,1)} %param.30) | copy-start | bytes 388
  14.0 49.5 %copy-start.28 = (bf16[192]{0:T(256)(128)(2,1)S(1)}, bf16[192]{0:T(256)(128)(2,1)}, u32[]{:S(2)}) copy-start(bf16[192]{0:T(256)(128)(2,1)} %param.35) | copy-start | bytes 1156
  14.0 132.9 %copy-start.20 = (bf16[128]{0:T(256)(128)(2,1)S(1)}, bf16[128]{0:T(256)(128)(2,1)}, u32[]{:S(2)}) copy-start(bf16[128]{0:T(256)(128)(2,1)} %param.37) | copy-start | bytes 772
  14.1 167.6 %copy-start.18 = (s32[1,169]{1,0:T(1,128)S(1)}, s32[1,169]{1,0:T(1,128)}, u32[]{:S(2)}) copy-start(s32[1,169]{1,0:T(1,128)} %param.27) | copy-start | bytes 2032
  14.1 167.6 %copy-start.19 = (s32[1,169]{1,0:T(1,128)S(1)}, s32[1,169]{1,0:T(1,128)}, u32[]{:S(2)}) copy-start(s32[1,169]{1,0:T(1,128)} %param.26) | copy-start | bytes 2032
  28.0 30.2 %collective-permute-start.2 = (bf16[128,4096]{1,0:T(8,128)(2,1)S(1)}, bf16[128,4096]{1,0:T(8,128)(2,1)}, u32[]{:S(2)}, u32[]{:S(2)}) collective-permute-start(bf16[128,4096]{1,0:T(8,128)(2,1)S(1)} %maximum_select_fusion.6), channel_id=1, source_target_pairs={{0,4},{1,5},{2,6},{3,7},{4,0},{5,1},{6,2},{7,3},{8,12},{9,13},{10,... | collective-permute-start | bytes 3145736 | tf_op jit(solution)/shard_map/ppermute | solution.py:23
  60.5 136.3 %collective-permute-start.3 = (bf16[256,4096]{1,0:T(8,128)(2,1)S(1)}, bf16[256,4096]{1,0:T(8,128)(2,1)}, u32[]{:S(2)}, u32[]{:S(2)}) collective-permute-start(bf16[256,4096]{1,0:T(8,128)(2,1)S(1)} %maximum_select_fusion.5), channel_id=1, source_target_pairs={{0,8},{1,9},{2,10},{3,11},{4,12},{5,13},{6,14},{7,15},{8,0},{9,1},... | collective-permute-start | bytes 6291464 | tf_op jit(solution)/shard_map/ppermute | solution.py:23
  201.7 209.6 %collective-permute-start.4 = (bf16[512,4096]{1,0:T(8,128)(2,1)}, bf16[512,4096]{1,0:T(8,128)(2,1)}, u32[]{:S(2)}, u32[]{:S(2)}) collective-permute-start(bf16[512,4096]{1,0:T(8,128)(2,1)} %maximum_select_fusion.4), channel_id=1, source_target_pairs={{0,16},{1,17},{2,18},{3,19},{4,20},{5,21},{6,22},{7,23},{8,24},{9,... | collective-permute-start | bytes 12582920 | tf_op jit(solution)/shard_map/ppermute | solution.py:23
  267.8 158.3 %copy-start.3 = (bf16[16,1,169,64]{2,3,1,0:T(8,128)(2,1)}, bf16[16,1,169,64]{2,3,1,0:T(8,128)(2,1)S(1)}, u32[]{:S(2)}) copy-start(bf16[16,1,169,64]{2,3,1,0:T(8,128)(2,1)S(1)} %get-tuple-element.138) | copy-start | bytes 1038340
  267.8 158.3 %copy-start.7 = (bf16[16,1,169,64]{3,2,1,0:T(8,128)(2,1)}, bf16[16,1,169,64]{3,2,1,0:T(8,128)(2,1)S(1)}, u32[]{:S(2)}) copy-start(bf16[16,1,169,64]{3,2,1,0:T(8,128)(2,1)S(1)} %get-tuple-element.785) | copy-start | bytes 1038340
  267.8 158.3 %copy-start.8 = (bf16[16,1,169,64]{3,2,1,0:T(8,128)(2,1)}, bf16[16,1,169,64]{3,2,1,0:T(8,128)(2,1)S(1)}, u32[]{:S(2)}) copy-start(bf16[16,1,169,64]{3,2,1,0:T(8,128)(2,1)S(1)} %get-tuple-element.786) | copy-start | bytes 1038340
  267.8 143.5 %copy-start.15 = (f32[32,1,128]{2,1,0:T(1,128)S(1)}, f32[32,1,128]{2,1,0:T(1,128)}, u32[]{:S(2)}) copy-start(f32[32,1,128]{2,1,0:T(1,128)} %convert_element_type.215) | copy-start | bytes 49156
  1357.4 149.8 %all-to-all-start.1 = ((bf16[4,32,12288]{2,1,0:T(8,128)(2,1)}), bf16[4,32,12288]{2,1,0:T(8,128)(2,1)}, u32[]{:S(2)}, u32[]{:S(2)}) async-start(bf16[4,32,12288]{2,1,0:T(8,128)(2,1)} %bitcast.257), calls=%async_computation.1 | async-start | bytes 6291456 | tf_op jit(solution)/shard_map/all_to_all | solution.py:249
  1362.1 133.6 %all-reduce.21.cloned.1.call-start = ((), (), s32[]{:S(2)}) async-start(), calls=%async_computation.6 | async-start | bytes 147456
  (19 other events, 181.1 us)
Sparse Core Ops, SparseCore 0:
  10.9 89.5 all-gather.5
  103.3 56.2 all-gather.7
  162.6 170.5 all-gather.9
  335.9 132.5 all-gather.11
  1369.7 126.0 all-reduce.20
